TPU v7x, 32 devices: a whole 2x2x4 slice. The times are simulated.
32 devices in a mesh: dp: 16 (over z, y, x), seq: 2 (over core).
Axes of the slice: x: 2, y: 2, z: 4, core: 2. Of those that a mesh axis runs over, the one named last changes fastest.
Arguments:
- tokens: bfloat16 [16, 2048, 1120], P('dp', 'seq'), may hold values from -6 to 6
- cotangent: bfloat16 [16, 2048, 1120], P('dp', 'seq'), may hold values from -6 to 6
- pad_mask: int32 [16, 2048], P('dp', 'seq'), may hold values from 0 to 1, as said below
- prefix_len: int32 [16], P('dp'), may hold values from 1 to 128
- norm_gains: float32 [2, 1120], replicated, may hold values from 0.5 to 1.5
- norm_shifts: float32 [2, 1120], replicated, may hold values from -1.8 to 1.8
- owner_map: int32 [192], replicated, may hold values from 0 to 191, as said below
- weight_copy: bfloat16 [192, 280, 280], P('dp'), may hold values from -1.8090681 to 1.8090681
- master: float32 [192, 280, 280], P('dp'), may hold values from -1.8090681 to 1.8090681
- average_weights: float32 [192, 280, 280], P('dp'), may hold values from -1.8090681 to 1.8090681
- stat_left: float32 [192, 280, 280], P('dp'), may hold values from -16.290909 to 36.654545, as said below
- stat_right: float32 [192, 280, 280], P('dp'), may hold values from -16.290909 to 36.654545, as said below
- root_left: float32 [192, 280, 280], P('dp'), may hold values from -3 to 5, as said below
- root_right: float32 [192, 280, 280], P('dp'), may hold values from -3 to 5, as said below
Outputs:
- block_out: bfloat16 [16, 2048, 1120], P('dp', 'seq')
- grad_input: float32 [16, 2048, 1120], P('dp', 'seq')
- norm_grad: float32 [4, 1120], replicated
- new_norms: float32 [4, 1120], replicated
- slot_grad: float32 [192, 280, 280], P('dp')
- new_left: float32 [192, 280, 280], P('dp')
- new_right: float32 [192, 280, 280], P('dp')
- new_master: float32 [192, 280, 280], P('dp')
- new_copy: bfloat16 [192, 280, 280], P('dp')
- new_average: float32 [192, 280, 280], P('dp')
Inputs may be any that keep to these rules, and one draw needn't show every extreme that they name: `pad_mask`: in each cell the ones come first, 512 or more of them; some cell has no zeros. `owner_map`: each block number appears once. `stat_left`: Symmetric. `stat_right`: Symmetric. `root_left`: Symmetric. `root_right`: Symmetric.
All inputs are finite; a program needn't handle non-finite values.
Results may differ from a plain program's by a relative error of at most 0.0085.
Values may be sent and summed in bfloat16 or wider, within the bound.
A program may use at most 448 MiB of HBM per device.

v0:
```python
import math
import jax
import jax.numpy as jnp
from jax import lax
from jax.sharding import PartitionSpec as P

HEADS = 20
GB = 256
PREFIX = 128
highest = lax.Precision.HIGHEST


def spread(block, axis, holder):
    block = jnp.where(lax.axis_index(axis) == holder, block, jnp.zeros_like(block))
    return lax.psum(block, axis)


def layer_norm(values, gain_row, shift_row):
    average = jnp.mean(values, axis=-1, keepdims=True)
    centred = values - average
    variance = jnp.mean(centred * centred, axis=-1, keepdims=True)
    return centred * lax.rsqrt(variance + 1e-05) * gain_row + shift_row


def gelu_tanh(values):
    return jax.nn.gelu(values, approximate=True)


def assemble(pieces, row_blocks, col_blocks):
    block_size = pieces.shape[-1]
    return (
        pieces.reshape(row_blocks, col_blocks, block_size, block_size)
        .transpose(0, 2, 1, 3)
        .reshape(row_blocks * block_size, col_blocks * block_size)
    )


def split_blocks(matrix, block_size):
    row_count, col_count = matrix.shape
    return (
        matrix.reshape(row_count // block_size, block_size, col_count // block_size, block_size)
        .transpose(0, 2, 1, 3)
        .reshape(-1, block_size, block_size)
    )


def matmul(left, right):
    return jnp.dot(left, right, preferred_element_type=jnp.float32)


def local(
    tokens,
    cotangent,
    pad_mask,
    prefix_len,
    norm_gains,
    norm_shifts,
    owner_map,
    weight_copy,
    master,
    average_weights,
    stat_left,
    stat_right,
    root_left,
    root_right,
):
    cell_count, group_len, features = tokens.shape
    row_count = cell_count * group_len
    head_size = features // HEADS
    per_group = group_len // GB
    score_scale = head_size ** (-0.5)
    slots = lax.all_gather(weight_copy, "dp", axis=0, tiled=True)
    block_count = slots.shape[0]
    block_size = slots.shape[-1]
    row_blocks = features // block_size
    col_blocks = (block_count - 4 * row_blocks * row_blocks) // (2 * row_blocks)
    square = row_blocks * row_blocks
    inverse = (
        jnp.zeros((block_count,), jnp.int32)
        .at[owner_map]
        .set(jnp.arange(block_count, dtype=jnp.int32))
    )
    blocks = jnp.take(slots, inverse, axis=0)
    w_query = assemble(blocks[0:square], row_blocks, row_blocks)
    w_key = assemble(blocks[square : 2 * square], row_blocks, row_blocks)
    w_value = assemble(blocks[2 * square : 3 * square], row_blocks, row_blocks)
    w_out = assemble(blocks[3 * square : 4 * square], row_blocks, row_blocks)
    w_up = assemble(
        blocks[4 * square : 4 * square + row_blocks * col_blocks], row_blocks, col_blocks
    )
    w_down = assemble(blocks[4 * square + row_blocks * col_blocks :], col_blocks, row_blocks)
    inputs = tokens.astype(jnp.float32).reshape(row_count, features)
    normed_one, norm_one_back = jax.vjp(layer_norm, inputs, norm_gains[0], norm_shifts[0])
    normed_in = normed_one.astype(jnp.bfloat16)
    queries = matmul(normed_in, w_query).astype(jnp.bfloat16)
    key_rows = matmul(normed_in, w_key).astype(jnp.bfloat16)
    value_rows = matmul(normed_in, w_value).astype(jnp.bfloat16)
    block_shape = (cell_count, per_group, GB, HEADS, head_size)
    query_blocks = queries.reshape(block_shape)
    key_blocks = key_rows.reshape(block_shape)
    value_blocks = value_rows.reshape(block_shape)
    key_cells = key_rows.reshape(cell_count, group_len, HEADS, head_size)
    value_cells = value_rows.reshape(cell_count, group_len, HEADS, head_size)
    prefix_keys, prefix_values = (
        spread(key_cells[:, :PREFIX], "seq", 0),
        spread(value_cells[:, :PREFIX], "seq", 0),
    )
    seq_index = lax.axis_index("seq")
    position = seq_index * group_len + jnp.arange(group_len, dtype=jnp.int32)
    alive_keys = jnp.where(
        position[None, :] < PREFIX, position[None, :] < prefix_len[:, None], pad_mask == 1
    )
    prefix_alive = jnp.arange(PREFIX, dtype=jnp.int32)[None, :] < prefix_len[:, None]
    offsets = jnp.arange(GB)
    local_seen = alive_keys.reshape(cell_count, per_group, 1, 1, GB) & (
        offsets[:, None] >= offsets[None, :]
    )
    later_block = seq_index * per_group + jnp.arange(per_group) > 0
    prefix_seen = prefix_alive[:, None, None, None, :] & later_block[None, :, None, None, None]
    visible = jnp.concatenate(
        [jnp.broadcast_to(prefix_seen, (cell_count, per_group, 1, GB, PREFIX)), local_seen], axis=-1
    )

    def score_rows():
        raw_prefix = jnp.einsum(
            "cnqhd,ckhd->cnhqk", query_blocks, prefix_keys, preferred_element_type=jnp.float32
        )
        raw_local = jnp.einsum(
            "cnqhd,cnkhd->cnhqk", query_blocks, key_blocks, preferred_element_type=jnp.float32
        )
        return jnp.where(
            visible, jnp.concatenate([raw_prefix, raw_local], axis=-1) * score_scale, -1e30
        )

    scores = score_rows()
    row_max = jnp.max(scores, axis=-1, keepdims=True)
    log_total = row_max + jnp.log(jnp.sum(jnp.exp(scores - row_max), axis=-1, keepdims=True))
    weights_low = jnp.exp(scores - log_total).astype(jnp.bfloat16)
    attended = jnp.einsum(
        "cnhqk,ckhd->cnqhd",
        weights_low[..., :PREFIX],
        prefix_values,
        preferred_element_type=jnp.float32,
    )
    attended = attended + jnp.einsum(
        "cnhqk,cnkhd->cnqhd",
        weights_low[..., PREFIX:],
        value_blocks,
        preferred_element_type=jnp.float32,
    )
    attended_low = attended.reshape(row_count, features).astype(jnp.bfloat16)
    middle = inputs + matmul(attended_low, w_out)
    normed_two, norm_two_back = jax.vjp(layer_norm, middle, norm_gains[1], norm_shifts[1])
    normed_mid = normed_two.astype(jnp.bfloat16)
    up_pre = matmul(normed_mid, w_up)
    activated, gelu_back = jax.vjp(gelu_tanh, up_pre)
    activated_low = activated.astype(jnp.bfloat16)
    block_out = (
        (middle + matmul(activated_low, w_down))
        .astype(jnp.bfloat16)
        .reshape(cell_count, group_len, features)
    )
    grad_rows = cotangent.astype(jnp.float32).reshape(row_count, features)
    grad_low = cotangent.reshape(row_count, features)
    grad_down = matmul(activated_low.T, grad_low)
    grad_act = matmul(grad_low, w_down.T)
    grad_pre = gelu_back(grad_act)[0].astype(jnp.bfloat16)
    grad_up = matmul(normed_mid.T, grad_pre)
    grad_mid_in = matmul(grad_pre, w_up.T)
    grad_middle_n, grad_gain_two, grad_shift_two = norm_two_back(grad_mid_in)
    grad_middle = grad_rows + grad_middle_n
    grad_branch = grad_middle.astype(jnp.bfloat16)
    grad_out = matmul(attended_low.T, grad_branch)
    grad_att = matmul(grad_branch, w_out.T).astype(jnp.bfloat16).reshape(block_shape)
    key_weights = jnp.exp(score_rows() - log_total)
    weights_again = key_weights.astype(jnp.bfloat16)
    grad_prob = jnp.concatenate(
        [
            jnp.einsum(
                "cnqhd,ckhd->cnhqk", grad_att, prefix_values, preferred_element_type=jnp.float32
            ),
            jnp.einsum(
                "cnqhd,cnkhd->cnhqk", grad_att, value_blocks, preferred_element_type=jnp.float32
            ),
        ],
        axis=-1,
    )
    grad_score = key_weights * (
        grad_prob - jnp.sum(key_weights * grad_prob, axis=-1, keepdims=True)
    )
    grad_raw = (grad_score * score_scale).astype(jnp.bfloat16)
    grad_raw_prefix = grad_raw[..., :PREFIX]
    grad_raw_local = grad_raw[..., PREFIX:]
    grad_query = jnp.einsum(
        "cnhqk,ckhd->cnqhd", grad_raw_prefix, prefix_keys, preferred_element_type=jnp.float32
    )
    grad_query = grad_query + jnp.einsum(
        "cnhqk,cnkhd->cnqhd", grad_raw_local, key_blocks, preferred_element_type=jnp.float32
    )
    grad_key = jnp.einsum(
        "cnhqk,cnqhd->cnkhd", grad_raw_local, query_blocks, preferred_element_type=jnp.float32
    )
    grad_value = jnp.einsum(
        "cnhqk,cnqhd->cnkhd",
        weights_again[..., PREFIX:],
        grad_att,
        preferred_element_type=jnp.float32,
    )
    grad_key_pre = jnp.einsum(
        "cnhqk,cnqhd->ckhd", grad_raw_prefix, query_blocks, preferred_element_type=jnp.float32
    )
    grad_value_pre = jnp.einsum(
        "cnhqk,cnqhd->ckhd",
        weights_again[..., :PREFIX],
        grad_att,
        preferred_element_type=jnp.float32,
    )
    summed_key, summed_value = lax.psum((grad_key_pre, grad_value_pre), "seq")
    is_owner = (seq_index == 0).astype(jnp.float32)
    grad_key = (
        grad_key.reshape(cell_count, group_len, features)
        .at[:, :PREFIX]
        .add(is_owner * summed_key.reshape(cell_count, PREFIX, features))
    )
    grad_value = (
        grad_value.reshape(cell_count, group_len, features)
        .at[:, :PREFIX]
        .add(is_owner * summed_value.reshape(cell_count, PREFIX, features))
    )
    query_grad_low = grad_query.reshape(row_count, features).astype(jnp.bfloat16)
    key_grad_low = grad_key.reshape(row_count, features).astype(jnp.bfloat16)
    value_grad_low = grad_value.reshape(row_count, features).astype(jnp.bfloat16)
    grad_wq = matmul(normed_in.T, query_grad_low)
    grad_wk = matmul(normed_in.T, key_grad_low)
    grad_wv = matmul(normed_in.T, value_grad_low)
    grad_normed = (
        matmul(query_grad_low, w_query.T)
        + matmul(key_grad_low, w_key.T)
        + matmul(value_grad_low, w_value.T)
    )
    grad_in_n, grad_gain_one, grad_shift_one = norm_one_back(grad_normed)
    grad_input = (grad_middle + grad_in_n).reshape(cell_count, group_len, features)
    grad_scale = 1.0 / math.sqrt(row_count * lax.axis_size("dp") * lax.axis_size("seq"))
    norm_terms = (
        jnp.stack([grad_gain_one, grad_shift_one, grad_gain_two, grad_shift_two]) * grad_scale
    )
    norm_grad = lax.psum(norm_terms, ("dp", "seq"))
    params = jnp.stack([norm_gains[0], norm_shifts[0], norm_gains[1], norm_shifts[1]])
    new_norms = params - 0.1 * norm_grad * lax.rsqrt(jnp.mean(norm_grad * norm_grad) + 1e-06)
    grad_blocks = (
        jnp.concatenate(
            [
                split_blocks(matrix, block_size)
                for matrix in (grad_wq, grad_wk, grad_wv, grad_out, grad_up, grad_down)
            ],
            axis=0,
        )
        * grad_scale
    )
    ordered = jnp.take(grad_blocks, owner_map, axis=0)
    owned_part = lax.psum_scatter(ordered, "dp", scatter_dimension=0, tiled=True)
    slot_grad = lax.psum(owned_part, "seq")
    new_left = (
        0.5 * stat_left
        + 0.5 * jnp.einsum("sij,skj->sik", slot_grad, slot_grad, precision=highest) / block_size
    )
    new_right = (
        0.5 * stat_right
        + 0.5 * jnp.einsum("sji,sjk->sik", slot_grad, slot_grad, precision=highest) / block_size
    )
    right_part = jnp.einsum("sij,sjk->sik", slot_grad, root_right, precision=highest)
    precond = jnp.einsum("sij,sjk->sik", root_left, right_part, precision=highest)
    new_master = master - 0.03 * precond
    new_copy = new_master.astype(jnp.bfloat16)
    new_average = 0.8 * average_weights + 0.2 * new_master
    return (
        block_out,
        grad_input,
        norm_grad,
        new_norms,
        slot_grad,
        new_left,
        new_right,
        new_master,
        new_copy,
        new_average,
    )


def solution(mesh):
    in_specs = (
        P("dp", "seq", None),
        P("dp", "seq", None),
        P("dp", "seq"),
        P("dp"),
        P(),
        P(),
        P(),
        P("dp", None, None),
        P("dp", None, None),
        P("dp", None, None),
        P("dp", None, None),
        P("dp", None, None),
        P("dp", None, None),
        P("dp", None, None),
    )
    out_specs = (
        P("dp", "seq", None),
        P("dp", "seq", None),
        P(),
        P(),
        P("dp", None, None),
        P("dp", None, None),
        P("dp", None, None),
        P("dp", None, None),
        P("dp", None, None),
        P("dp", None, None),
    )
    return jax.shard_map(local, mesh=mesh, in_specs=in_specs, out_specs=out_specs, check_vma=False)
```

profile of v0, /device:TPU:0, one launch (start us, length us, event | category | flops | bytes accessed | tf_op | source)
XLA Modules:
  0.0 2638.7 jit_solution(1818044440257464110)
XLA Ops:
  16.7 420.8 %all-gather.2.cloned.1.call-done = bf16[192,280,280]{2,1,0:T(8,128)(2,1)} async-done(((bf16[12,280,280]{2,1,0:T(8,128)(2,1)}), bf16[192,280,280]{2,1,0:T(8,128)(2,1)}) %all-gather.2.cloned.1.call-update) | async-done | bytes 30105616 | tf_op jit(solution)/shard_map/all_gather | solution.py:72
  437.5 28.3 %gather_fusion = bf16[192,280,280]{2,1,0:T(8,128)(2,1)} fusion(bf16[192,280,280]{2,1,0:T(8,128)(2,1)} %all-gather.2.cloned.1.call-done, s32[1024]{0:T(1024)S(1)} %pad_clamp_fusion.1), kind=kCustom, calls=%fused_computation | custom fusion | bytes 60211968 | tf_op jit(solution)/shard_map/jit(_take)/gather | solution.py:83
  465.8 28.1 %broadcast_select_fusion.1 = bf16[192,280,280]{2,1,0:T(8,128)(2,1)} fusion(bf16[192,280,280]{2,1,0:T(8,128)(2,1)} %gather_fusion, pred[192]{0:T(512)(128)(4,1)S(1)} %compare_and_fusion.1), kind=kLoop, calls=%fused_computation.5 | loop fusion | flops 15052800 | bytes 60211392 | tf_op jit(solution)/shard_map/jit(_take)/select_n | solution.py:83
  503.2 21.0 fusion.110
  601.5 22.4 copy.115
  623.9 21.1 reshape.779
  644.9 14.3 copy.247
  659.3 21.4 reshape.777
  680.7 11.6 convolution_bitcast_fusion.1
  695.0 13.9 fusion.108
  716.3 9.9 fusion.1
  741.5 26.2 fusion.16
  767.8 31.0 %fusion.8 = bf16[1024,4480]{1,0:T(8,128)(2,1)} fusion(f32[1024,4480]{1,0:T(8,128)} %get-tuple-element.100, bf16[4480,1120]{0,1:T(8,128)(2,1)} %reshape.779, bf16[1,1024,1120]{1,2,0:T(8,128)(2,1)S(1)} %copy-done.12), kind=kOutput, calls=%fused_computation.23 | convolution fusion | flops 10367795200 | bytes 39854080 | tf_op jit(solution)/shard_map/dot_general | solution.py:48
  798.8 19.8 multiply_reduce_fusion.1
  861.1 20.7 multiply_reduce_fusion
  881.8 22.1 multiply_convert_fusion
  930.5 18.1 fusion.103
  988.5 28.5 %reshape.801 = f32[4,280,16,280]{3,2,1,0:T(8,128)} reshape(f32[1120,4480]{1,0:T(8,128)} %fusion.103) | data formatting | bytes 40140800 | tf_op jit(solution)/shard_map/reshape | solution.py:41
  1017.1 27.0 %copy.138 = f32[4,280,16,280]{3,1,2,0:T(8,128)} copy(f32[4,280,16,280]{3,2,1,0:T(8,128)} %reshape.801) | data formatting | bytes 40140800 | tf_op jit(solution)/shard_map/reshape | solution.py:41
  1044.0 12.7 copy.139
  1056.8 20.0 fusion.117
  1155.3 20.5 constant_dynamic-update-slice_fusion
  1175.8 55.9 %broadcast_multiply_fusion = f32[192,280,280]{2,1,0:T(8,128)} fusion(f32[192,280,280]{2,1,0:T(8,128)} %constant_dynamic-update-slice_fusion), kind=kLoop, calls=%fused_computation.4 | loop fusion | flops 15052800 | bytes 120422400 | tf_op jit(solution)/shard_map/mul | solution.py:251
  1231.7 56.4 %gather_fusion.1 = f32[192,280,280]{2,1,0:T(8,128)} fusion(f32[192,280,280]{2,1,0:T(8,128)} %broadcast_multiply_fusion, s32[1024]{0:T(1024)} %pad_clamp_fusion), kind=kCustom, calls=%fused_computation.1 | custom fusion | bytes 120423168 | tf_op jit(solution)/shard_map/jit(_take)/gather | solution.py:260
  1288.1 54.1 %broadcast_select_fusion = f32[192,280,280]{2,1,0:T(8,128)} fusion(f32[192,280,280]{2,1,0:T(8,128)} %gather_fusion.1, pred[192]{0:T(512)(128)(4,1)S(1)} %copy-done.57), kind=kLoop, calls=%fused_computation.3 | loop fusion | flops 15052800 | bytes 120422592 | tf_op jit(solution)/shard_map/jit(_take)/select_n | solution.py:260
  1342.2 1134.6 %reduce-scatter.2.cloned.1.call-done = f32[12,280,280]{2,1,0:T(8,128)} async-done(((f32[192,280,280]{2,1,0:T(8,128)}), f32[12,280,280]{2,1,0:T(8,128)}) %reduce-scatter.2.cloned.1.call-update) | async-done | bytes 3763216 | tf_op jit(solution)/shard_map/reduce_scatter | solution.py:261
  2489.6 19.8 fusion.54
  2509.4 39.9 %psum.46 = f32[4,1120]{1,0:T(4,128)S(1)} all-reduce(f32[4,1120]{1,0:T(4,128)S(1)} %maximum_multiply_fusion.1), channel_id=1, replica_groups=mesh['dp'=16,'seq'=2] {'dp','seq'}, use_global_device_ids=true, to_apply=%region_20.21 | all-reduce | flops 4480 | bytes 35840 | tf_op jit(solution)/shard_map/psum | solution.py:247
  2551.3 14.1 fusion.118
  2565.4 17.3 multiply_add_fusion
  2597.8 16.9 multiply_add_fusion.2
  2614.7 14.9 multiply_add_fusion.1
  (290 shorter events, 339.0 us)
Async XLA Ops:
  7.2 430.3 %all-gather.2.cloned.1.call-start = ((), (), s32[]{:S(2)}) async-start(), calls=%async_computation.1 | async-start | bytes 43868160 | tf_op jit(solution)/shard_map/all_gather | solution.py:72
  7.9 684.3 %all-reduce.10.cloned.1.call-start = ((), (), s32[]{:S(2)}) async-start(), calls=%async_computation.5 | async-start | bytes 1146880 | tf_op jit(solution)/shard_map/psum | solution.py:15
  14.2 555.5 %copy-start.34 = (f32[1024]{0:T(1024)}, f32[1024]{0:T(1024)S(1)}, u32[]{:S(2)}) copy-start(f32[1024]{0:T(1024)S(1)} %broadcast_multiply_fusion.4) | copy-start | bytes 12292
  15.5 554.3 %copy-start.40 = (f32[1024]{0:T(1024)}, f32[1024]{0:T(1024)S(1)}, u32[]{:S(2)}) copy-start(f32[1024]{0:T(1024)S(1)} %fusion.95) | copy-start | bytes 12292
  16.7 553.0 %copy-start.32 = (f32[1120]{0:T(1024)}, f32[1120]{0:T(1024)S(1)}, u32[]{:S(2)}) copy-start(f32[1120]{0:T(1024)S(1)} %get-tuple-element.104) | copy-start | bytes 13444
  16.7 553.0 %copy-start.42 = (f32[1120]{0:T(1024)}, f32[1120]{0:T(1024)S(1)}, u32[]{:S(2)}) copy-start(f32[1120]{0:T(1024)S(1)} %get-tuple-element.73) | copy-start | bytes 13444
  569.7 517.7 %all-reduce.8.cloned.1.call-start = ((), (), s32[]{:S(2)}) async-start(), calls=%async_computation.4 | async-start | bytes 2293760 | tf_op jit(solution)/shard_map/psum | solution.py:218
  589.3 103.0 %copy-start.2 = (bf16[4,256,20,56]{1,0,3,2:T(4,128)(2,1)}, bf16[4,256,20,56]{1,0,3,2:T(4,128)(2,1)S(1)}, u32[]{:S(2)}) copy-start(bf16[4,256,20,56]{1,0,3,2:T(4,128)(2,1)S(1)} %reshape.769) | copy-start | bytes 6881284
  695.0 21.3 copy-start
  740.9 77.7 %copy-start.8 = (f32[1024,1120]{0,1:T(8,128)}, f32[1024,1120]{0,1:T(8,128)S(1)}, u32[]{:S(2)}) copy-start(f32[1024,1120]{0,1:T(8,128)S(1)} %get-tuple-element.95) | copy-start | bytes 13762564
  741.5 26.3 copy-start.12
  881.8 27.6 %copy-start.3 = (bf16[4,256,20,56]{1,0,3,2:T(4,128)(2,1)S(1)}, bf16[4,256,20,56]{1,0,3,2:T(4,128)(2,1)}, u32[]{:S(2)}) copy-start(bf16[4,256,20,56]{1,0,3,2:T(4,128)(2,1)} %copy-done.2) | copy-start | bytes 6881284
  912.1 18.3 slice-start.16
  920.8 27.8 %slice-start.18 = ((s8[4587520]{0:T(1024)(128)(4,1)}), s8[4194304]{0:T(1024)(128)(4,1)S(1)}, s32[]{:S(2)}) async-start(s8[4587520]{0:T(1024)(128)(4,1)} %bitcast.354), calls=%async_computation.24 | async-start | bytes 8388608
  930.4 18.1 slice-start.19
  1056.7 1420.1 %reduce-scatter.2.cloned.1.call-start = ((), (), s32[]{:S(2)}) async-start(), calls=%async_computation.2 | async-start | bytes 87736320 | tf_op jit(solution)/shard_map/reduce_scatter | solution.py:261
  1056.8 20.0 copy-start.17
  1056.8 20.0 copy-start.22
  1121.3 24.5 slice-start.7
  1121.3 24.5 slice-start.8
  1121.3 24.5 slice-start.9
  1128.9 16.9 slice-start.10
  1231.7 56.4 %copy-start.57 = (pred[192]{0:T(512)(128)(4,1)S(1)}, pred[192]{0:T(512)(128)(4,1)}, u32[]{:S(2)}) copy-start(pred[192]{0:T(512)(128)(4,1)} %compare_and_fusion) | copy-start | bytes 580
  1342.2 1209.1 %all-reduce.6.cloned.1.call-start = ((), (), s32[]{:S(2)}) async-start(), calls=%async_computation.3 | async-start | bytes 10321920 | tf_op jit(solution)/shard_map/psum | solution.py:262
  2489.5 19.9 copy-start.46
  2489.5 19.9 copy-start.45
  2489.5 61.1 %copy-start.47 = (f32[1,1120]{1,0:T(1,128)S(1)}, f32[1,1120]{1,0:T(1,128)}, u32[]{:S(2)}) copy-start(f32[1,1120]{1,0:T(1,128)} %get-tuple-element.91) | copy-start | bytes 13444
  2489.5 61.1 %copy-start.48 = (f32[1,1120]{1,0:T(1,128)S(1)}, f32[1,1120]{1,0:T(1,128)}, u32[]{:S(2)}) copy-start(f32[1,1120]{1,0:T(1,128)} %get-tuple-element.93) | copy-start | bytes 13444
  2489.5 61.1 %copy-start.49 = (f32[1,1120]{1,0:T(1,128)S(1)}, f32[1,1120]{1,0:T(1,128)}, u32[]{:S(2)}) copy-start(f32[1,1120]{1,0:T(1,128)} %get-tuple-element.102) | copy-start | bytes 13444
  2489.6 61.1 %copy-start.50 = (f32[1,1120]{1,0:T(1,128)S(1)}, f32[1,1120]{1,0:T(1,128)}, u32[]{:S(2)}) copy-start(f32[1,1120]{1,0:T(1,128)} %get-tuple-element.103) | copy-start | bytes 13444
  2591.6 23.1 slice-start.5
  2597.8 16.9 slice-start.6
  (55 other events, 397.7 us)
Sparse Core Ops, SparseCore 0:
  10.8 426.5 all-gather.1
  569.8 17.0 all-reduce.9
  1056.8 18.0 all-reduce.7
  1342.3 1134.4 reduce-scatter.1
  2479.3 29.0 all-reduce.5
where the time goes:
time: 2650 us; the launch traced here: 2640 us
  waiting for transfers between devices  1560 us (59%)
  local copies, waits for them, and re-layouts  452 us (17%)
  matrix products  338 us (13%)
  other arithmetic  236 us (9%)
  blocking collectives  39.9 us (2%)
    reduce_scatter x1, waiting for transfers between devices, local(): lax.psum_scatter(ordered, 'dp', scatter_dimension=0, tiled=True)  1130 us
    all_gather x1, waiting for transfers between devices, local(): slots = lax.all_gather(weight_copy, 'dp', axis=0, tiled=True)  421 us
    dot_general x18, matrix products, matmul(): return jnp.dot(left, right, preferred_element_type=jnp.float32)  197 us
    unnamed x179, local copies, waits for them, and re-layouts  81.6 us
    reshape x6, local copies, waits for them, and re-layouts, assemble(): return pieces.reshape(row_blocks, col_blocks, block_size, block_size).tra...  67.7 us
    gather x1, local copies, waits for them, and re-layouts, local(): ordered = jnp.take(grad_blocks, owner_map, axis=0)  56.4 us
    mul x1, other arithmetic, local(): jnp.concatenate([split_blocks(matrix, block_size) for matrix in (grad_wq,...  55.9 us
    reshape x2, local copies, waits for them, and re-layouts, split_blocks(): matrix.reshape(row_count // block_size, block_size, col_count // block_si...  55.5 us
  transfers between devices with their start and end apart: 5, of which 2 were waited for; matrix products, arithmetic and copies ran while one was open for 7% of the time, Pallas kernels for 0%

commit v1 on v0

--- a/solution.py
+++ b/solution.py
@@ -8,6 +8,21 @@
 GB = 256
 PREFIX = 128
 highest = lax.Precision.HIGHEST
+
+
+def detail_column_now(xx, bus_axis):
+    mat_out, block_last, g_now = (lax.axis_size(bus_axis), lax.axis_index(bus_axis), xx.shape[0])
+    a_now, f_next = (xx, 1)
+    while f_next < mat_out:
+        sheets = []
+        w = 0
+        while w < mat_out:
+            sheets.append((w, (w - f_next) % mat_out))
+            w += 1
+        a_now = jnp.concatenate([a_now, lax.ppermute(a_now, bus_axis, sheets)], axis=0)
+        f_next = 2 * f_next
+    y_new = jnp.roll(a_now, block_last * g_now, axis=0)
+    return y_new
 
 
 def spread(block, axis, holder):
@@ -69,7 +84,7 @@
     head_size = features // HEADS
     per_group = group_len // GB
     score_scale = head_size ** (-0.5)
-    slots = lax.all_gather(weight_copy, "dp", axis=0, tiled=True)
+    slots = detail_column_now(weight_copy, "dp")
     block_count = slots.shape[0]
     block_size = slots.shape[-1]
     row_blocks = features // block_size

time: 2650 us -> 3650 us (1.38)
  waiting for transfers between devices: 1560 us -> 2370 us
  local copies, waits for them, and re-layouts: 452 us -> 607 us
    ppermute x0 -> x4, waiting for transfers between devices: none -> 1230 us  [detail_column_now(): lax.ppermute(a_now, bus_axis, sheets)]
    all_gather x1 -> x0, waiting for transfers between devices: 421 us -> none  [local(): slots = lax.all_gather(weight_copy, 'dp', axis=0, tiled=True)]
    reshape x6 -> x0, local copies, waits for them, and re-layouts: 53.9 us -> none  [assemble(): pieces.reshape(row_blocks, col_blocks, block_size, block_size)]
    transpose x0 -> x6, local copies, waits for them, and re-layouts: none -> 52.4 us  [assemble(): return pieces.reshape(row_blocks, col_blocks, block_size, block_size).tra...]
    unnamed x179 -> x218, local copies, waits for them, and re-layouts: 81.6 us -> 134 us
    concatenate x0 -> x2, local copies, waits for them, and re-layouts: none -> 47.9 us  [the longest x1 30.5 us: detail_column_now(): jnp.concatenate([a_now, lax.ppermute(a_now, bus_axis, sheets)], axis=0)]
  transfers between devices with their start and end apart: 5 -> 8, of which waited for: 2 -> 5; matrix products, arithmetic and copies ran while one was open for 7% -> 6% of each run, Pallas kernels for 0% -> 0%
where the time goes in v1:
time: 3650 us; the launch traced here: 3630 us
  waiting for transfers between devices  2370 us (65%)
  local copies, waits for them, and re-layouts  607 us (17%)
  matrix products  338 us (9%)
  other arithmetic  257 us (7%)
  blocking collectives  39.8 us (1%)
    ppermute x4, waiting for transfers between devices, detail_column_now(): lax.ppermute(a_now, bus_axis, sheets)  1230 us
    reduce_scatter x1, waiting for transfers between devices, local(): lax.psum_scatter(ordered, 'dp', scatter_dimension=0, tiled=True)  1140 us
    dot_general x18, matrix products, matmul(): return jnp.dot(left, right, preferred_element_type=jnp.float32)  197 us
    unnamed x218, local copies, waits for them, and re-layouts  134 us
  transfers between devices with their start and end apart: 8, of which 5 were waited for; matrix products, arithmetic and copies ran while one was open for 6% of the time, Pallas kernels for 0%

profile of v1, /device:TPU:0, one launch (start us, length us, event | category | flops | bytes accessed | tf_op | source)
XLA Modules:
  0.0 3634.4 jit_solution(9172140450231348548)
XLA Ops:
  14.2 55.6 %collective-permute-done = bf16[12,280,280]{2,1,0:T(8,128)(2,1)S(1)} collective-permute-done((bf16[12,280,280]{2,1,0:T(8,128)(2,1)}, bf16[12,280,280]{2,1,0:T(8,128)(2,1)S(1)}, u32[]{:S(2)}, u32[]{:S(2)}) %collective-permute-start) | collective-permute-done | bytes 1881632 | tf_op jit(solution)/shard_map/ppermute | solution.py:22
  74.8 110.7 %collective-permute-done.1 = bf16[24,280,280]{2,1,0:T(8,128)(2,1)S(1)} collective-permute-done((bf16[24,280,280]{2,1,0:T(8,128)(2,1)S(1)}, bf16[24,280,280]{2,1,0:T(8,128)(2,1)S(1)}, u32[]{:S(2)}, u32[]{:S(2)}) %collective-permute-start.1) | collective-permute-done | bytes 3763232 | tf_op jit(solution)/shard_map/ppermute | solution.py:22
  188.1 221.3 %collective-permute-done.2 = bf16[48,280,280]{2,1,0:T(8,128)(2,1)S(1)} collective-permute-done((bf16[48,280,280]{2,1,0:T(8,128)(2,1)S(1)}, bf16[48,280,280]{2,1,0:T(8,128)(2,1)S(1)}, u32[]{:S(2)}, u32[]{:S(2)}) %collective-permute-start.2) | collective-permute-done | bytes 7526432 | tf_op jit(solution)/shard_map/ppermute | solution.py:22
  428.4 30.5 copy.153
  481.5 838.1 %collective-permute-done.3 = bf16[96,280,280]{0,2,1:T(8,128)(2,1)} collective-permute-done((bf16[96,280,280]{0,2,1:T(8,128)(2,1)}, bf16[96,280,280]{0,2,1:T(8,128)(2,1)}, u32[]{:S(2)}, u32[]{:S(2)}) %collective-permute-start.3) | collective-permute-done | bytes 15052832 | tf_op jit(solution)/shard_map/ppermute | solution.py:22
  1319.7 31.6 copy.154
  1351.3 17.7 constant_dynamic-update-slice_fusion.5
  1384.9 17.4 constant_dynamic-update-slice_fusion
  1402.3 28.0 constant_dynamic-slice_fusion
  1430.3 28.1 gather_fusion
  1458.4 28.2 broadcast_select_fusion.1
  1496.0 21.0 fusion.110
  1590.4 22.5 copy.170
  1612.9 21.1 reshape.779
  1648.3 21.5 reshape.777
  1730.7 26.3 fusion.16
  1756.9 30.9 fusion.8
  1787.9 19.8 multiply_reduce_fusion.1
  1850.2 20.7 multiply_reduce_fusion
  1870.9 22.1 multiply_convert_fusion
  1919.5 18.5 fusion.103
  1977.9 28.5 reshape.801
  2006.4 27.0 copy.193
  2046.2 19.9 fusion.117
  2144.5 20.7 constant_dynamic-update-slice_fusion.10
  2165.1 56.0 %broadcast_multiply_fusion = f32[192,280,280]{2,1,0:T(8,128)} fusion(f32[192,280,280]{2,1,0:T(8,128)} %constant_dynamic-update-slice_fusion.10), kind=kLoop, calls=%fused_computation.4 | loop fusion | flops 15052800 | bytes 120422400 | tf_op jit(solution)/shard_map/mul | solution.py:266
  2221.2 56.3 %gather_fusion.1 = f32[192,280,280]{2,1,0:T(8,128)} fusion(f32[192,280,280]{2,1,0:T(8,128)} %broadcast_multiply_fusion, s32[1024]{0:T(1024)} %pad_clamp_fusion), kind=kCustom, calls=%fused_computation.1 | custom fusion | bytes 120423168 | tf_op jit(solution)/shard_map/jit(_take)/gather | solution.py:275
  2277.5 54.2 %broadcast_select_fusion = f32[192,280,280]{2,1,0:T(8,128)} fusion(f32[192,280,280]{2,1,0:T(8,128)} %gather_fusion.1, pred[192]{0:T(512)(128)(4,1)S(1)} %copy-done.68), kind=kLoop, calls=%fused_computation.3 | loop fusion | flops 15052800 | bytes 120422592 | tf_op jit(solution)/shard_map/jit(_take)/select_n | solution.py:275
  2331.7 1140.8 %reduce-scatter.2.cloned.1.call-done = f32[12,280,280]{2,1,0:T(8,128)} async-done(((f32[192,280,280]{2,1,0:T(8,128)}), f32[12,280,280]{2,1,0:T(8,128)}) %reduce-scatter.2.cloned.1.call-update) | async-done | bytes 3763216 | tf_op jit(solution)/shard_map/reduce_scatter | solution.py:276
  3485.3 19.8 fusion.54
  3505.2 39.8 %psum.46 = f32[4,1120]{1,0:T(4,128)S(1)} all-reduce(f32[4,1120]{1,0:T(4,128)S(1)} %maximum_multiply_fusion.1), channel_id=1, replica_groups=mesh['dp'=16,'seq'=2] {'dp','seq'}, use_global_device_ids=true, to_apply=%region_20.21 | all-reduce | flops 4480 | bytes 35840 | tf_op jit(solution)/shard_map/psum | solution.py:262
  3561.1 17.3 multiply_add_fusion
  (342 shorter events, 506.0 us)
Async XLA Ops:
  7.2 178.4 %copy-start.4 = (bf16[12,280,280]{2,1,0:T(8,128)(2,1)S(1)}, bf16[12,280,280]{2,1,0:T(8,128)(2,1)}, u32[]{:S(2)}) copy-start(bf16[12,280,280]{2,1,0:T(8,128)(2,1)} %param.25) | copy-start | bytes 5644804
  7.2 1674.2 %all-reduce.10.cloned.1.call-start = ((), (), s32[]{:S(2)}) async-start(), calls=%async_computation.4 | async-start | bytes 1146880 | tf_op jit(solution)/shard_map/psum | solution.py:30
  7.2 62.5 %collective-permute-start = (bf16[12,280,280]{2,1,0:T(8,128)(2,1)}, bf16[12,280,280]{2,1,0:T(8,128)(2,1)S(1)}, u32[]{:S(2)}, u32[]{:S(2)}) collective-permute-start(bf16[12,280,280]{2,1,0:T(8,128)(2,1)} %param.25), channel_id=1, source_target_pairs={{0,30},{2,0},{4,2},{6,4},{8,6},{10,8},{12,10},{14,12},{16,14},{18,... | collective-permute-start | bytes 5644808 | tf_op jit(solution)/shard_map/ppermute | solution.py:22
  69.8 339.7 %copy-start.5 = (bf16[12,280,280]{2,1,0:T(8,128)(2,1)}, bf16[12,280,280]{2,1,0:T(8,128)(2,1)S(1)}, u32[]{:S(2)}) copy-start(bf16[12,280,280]{2,1,0:T(8,128)(2,1)S(1)} %collective-permute-done) | copy-start | bytes 5644804
  73.3 112.2 %collective-permute-start.1 = (bf16[24,280,280]{2,1,0:T(8,128)(2,1)S(1)}, bf16[24,280,280]{2,1,0:T(8,128)(2,1)S(1)}, u32[]{:S(2)}, u32[]{:S(2)}) collective-permute-start(bf16[24,280,280]{2,1,0:T(8,128)(2,1)S(1)} %pad_maximum_fusion.3), channel_id=1, source_target_pairs={{0,28},{2,30},{4,0},{6,2},{8,4},{10,6},{12,8},{14,10},{16,12},{18,... | collective-permute-start | bytes 11289608 | tf_op jit(solution)/shard_map/ppermute | solution.py:22
  185.5 223.9 %copy-start.3 = (bf16[24,280,280]{2,1,0:T(8,128)(2,1)}, bf16[24,280,280]{2,1,0:T(8,128)(2,1)S(1)}, u32[]{:S(2)}) copy-start(bf16[24,280,280]{2,1,0:T(8,128)(2,1)S(1)} %collective-permute-done.1) | copy-start | bytes 11289604
  187.6 221.9 %collective-permute-start.2 = (bf16[48,280,280]{2,1,0:T(8,128)(2,1)S(1)}, bf16[48,280,280]{2,1,0:T(8,128)(2,1)S(1)}, u32[]{:S(2)}, u32[]{:S(2)}) collective-permute-start(bf16[48,280,280]{2,1,0:T(8,128)(2,1)S(1)} %pad_maximum_fusion.2), channel_id=1, source_target_pairs={{0,24},{2,26},{4,28},{6,30},{8,0},{10,2},{12,4},{14,6},{16,8},{18,... | collective-permute-start | bytes 22579208 | tf_op jit(solution)/shard_map/ppermute | solution.py:22
  428.4 31.2 copy-start.67
  428.4 31.2 copy-start.66
  458.9 860.8 %collective-permute-start.3 = (bf16[96,280,280]{0,2,1:T(8,128)(2,1)}, bf16[96,280,280]{0,2,1:T(8,128)(2,1)}, u32[]{:S(2)}, u32[]{:S(2)}) collective-permute-start(bf16[96,280,280]{0,2,1:T(8,128)(2,1)} %copy.153), channel_id=1, source_target_pairs={{0,16},{2,18},{4,20},{6,22},{8,24},{10,26},{12,28},{14,30},{16,0},... | collective-permute-start | bytes 45158408 | tf_op jit(solution)/shard_map/ppermute | solution.py:22
  1319.7 53.7 %slice-start.16 = ((s8[5160960]{0:T(1024)(128)(4,1)}), s8[966656]{0:T(1024)(128)(4,1)S(1)}, s32[]{:S(2)}) async-start(s8[5160960]{0:T(1024)(128)(4,1)} %bitcast.341), calls=%async_computation.21 | async-start | bytes 1933312
  1351.3 22.2 slice-start.17
  1558.3 518.3 %all-reduce.8.cloned.1.call-start = ((), (), s32[]{:S(2)}) async-start(), calls=%async_computation.3 | async-start | bytes 2293760 | tf_op jit(solution)/shard_map/psum | solution.py:233
  1578.1 103.2 %copy-start.8 = (bf16[4,256,20,56]{1,0,3,2:T(4,128)(2,1)}, bf16[4,256,20,56]{1,0,3,2:T(4,128)(2,1)S(1)}, u32[]{:S(2)}) copy-start(bf16[4,256,20,56]{1,0,3,2:T(4,128)(2,1)S(1)} %reshape.769) | copy-start | bytes 6881284
  1684.1 21.4 copy-start
  1730.1 77.6 %copy-start.15 = (f32[1024,1120]{0,1:T(8,128)}, f32[1024,1120]{0,1:T(8,128)S(1)}, u32[]{:S(2)}) copy-start(f32[1024,1120]{0,1:T(8,128)S(1)} %get-tuple-element.105) | copy-start | bytes 13762564
  1730.7 26.3 copy-start.20
  1870.9 27.6 copy-start.9
  1909.9 28.1 slice-start.22
  2046.1 1426.3 %reduce-scatter.2.cloned.1.call-start = ((), (), s32[]{:S(2)}) async-start(), calls=%async_computation.1 | async-start | bytes 87736320 | tf_op jit(solution)/shard_map/reduce_scatter | solution.py:276
  2046.2 20.0 copy-start.25
  2046.2 19.9 copy-start.30
  2110.5 24.5 slice-start.7
  2110.5 24.5 slice-start.8
  2110.6 24.5 slice-start.9
  2221.2 56.3 %copy-start.68 = (pred[192]{0:T(512)(128)(4,1)S(1)}, pred[192]{0:T(512)(128)(4,1)}, u32[]{:S(2)}) copy-start(pred[192]{0:T(512)(128)(4,1)} %get-tuple-element.116) | copy-start | bytes 580
  2331.7 1215.3 %all-reduce.6.cloned.1.call-start = ((), (), s32[]{:S(2)}) async-start(), calls=%async_computation.2 | async-start | bytes 10321920 | tf_op jit(solution)/shard_map/psum | solution.py:277
  3485.3 61.1 %copy-start.56 = (f32[1,1120]{1,0:T(1,128)S(1)}, f32[1,1120]{1,0:T(1,128)}, u32[]{:S(2)}) copy-start(f32[1,1120]{1,0:T(1,128)} %get-tuple-element.101) | copy-start | bytes 13444
  3485.3 61.1 %copy-start.57 = (f32[1,1120]{1,0:T(1,128)S(1)}, f32[1,1120]{1,0:T(1,128)}, u32[]{:S(2)}) copy-start(f32[1,1120]{1,0:T(1,128)} %get-tuple-element.103) | copy-start | bytes 13444
  3485.3 61.1 %copy-start.58 = (f32[1,1120]{1,0:T(1,128)S(1)}, f32[1,1120]{1,0:T(1,128)}, u32[]{:S(2)}) copy-start(f32[1,1120]{1,0:T(1,128)} %get-tuple-element.112) | copy-start | bytes 13444
  3485.3 61.1 %copy-start.59 = (f32[1,1120]{1,0:T(1,128)S(1)}, f32[1,1120]{1,0:T(1,128)}, u32[]{:S(2)}) copy-start(f32[1,1120]{1,0:T(1,128)} %get-tuple-element.113) | copy-start | bytes 13444
  3587.3 23.2 slice-start.5
  (73 other events, 585.4 us)
Sparse Core Ops, SparseCore 0:
  1558.4 23.6 all-reduce.9
  2046.3 24.5 all-reduce.7
  2331.8 1140.6 reduce-scatter.1
  3475.0 28.9 all-reduce.5
